TPU v7x, 32 devices: a whole 2x2x4 slice. The times are simulated.
32 devices in a mesh: pipe: 8 (over y, x, core), dp: 4 (over z).
Axes of the slice: x: 2, y: 2, z: 4, core: 2. Of those that a mesh axis runs over, the one named last changes fastest.
Arguments:
- inputs: bfloat16 [8, 1024, 1024], P('pipe', 'dp'), may hold values from -6 to 6
- cotangents: bfloat16 [8, 1024, 512], P('pipe', 'dp'), may hold values from -0.09375 to 0.09375
- input_factors: float32 [8, 1024, 256], P('pipe', 'dp'), may hold values from -20 to 20, as said below
- output_factors: float32 [8, 512, 512], P('pipe'), may hold values from -20 to 20, as said below
- input_coupling: float32 [8, 1024, 256], P('pipe', 'dp'), may hold values from -0.375 to 0.375
- output_coupling: float32 [8, 512, 512], P('pipe'), may hold values from -0.25 to 0.25
Outputs:
- update: float32 [8, 1024, 512], P('pipe', 'dp')
Inputs may be any that keep to these rules, and one draw needn't show every extreme that they name: Each [256, 256] row block of a layer's input_factors is positive definite. Each layer's output_factors is positive definite.
All inputs are finite; a program needn't handle non-finite values. Where the computation divides by a largest or mean magnitude, that divisor is 1e-20 or more.
Results may differ from a plain program's by a relative error of at most 0.0003.
Values may be sent and summed in bfloat16 or wider, within the bound.
A program may use at most 64 MiB of HBM per device.

v0:
```python
import jax
import jax.numpy as jnp
from jax import lax
from jax.sharding import PartitionSpec as P

NS_ITERS = 2


def passed_along(value, axis, steps):
    count = lax.axis_size(axis)
    first, last = (max(0, -steps), min(count, count - steps))
    return lax.ppermute(value, axis, [(source, source + steps) for source in range(first, last)])


def matmul(left, right):
    return jnp.matmul(left, right, precision=lax.Precision.HIGHEST)


def invert(factor):
    order = factor.shape[-1]
    identity = jnp.eye(order, dtype=jnp.float32)
    bound_value = jnp.max(jnp.sum(jnp.abs(factor), axis=1))
    iterate = identity / bound_value
    for sweep in range(NS_ITERS):
        iterate = matmul(iterate, 2.0 * identity - matmul(factor, iterate))
    return iterate


def contract_tokens(left, right):
    return lax.dot_general(
        left, right, (((0,), (0,)), ((), ())), preferred_element_type=jnp.float32
    )


def shards(inputs, cotangents, input_factors, output_factors, input_coupling, output_coupling):
    panel_rows = inputs[0]
    cotangent_block = cotangents[0]
    columns = lax.all_to_all(panel_rows, "dp", split_axis=1, concat_axis=0, tiled=True)
    gradient = contract_tokens(columns, lax.all_gather(cotangent_block, "dp", axis=0, tiled=True))
    coupling_block = input_coupling[0]
    coupling_out = output_coupling[0]
    following = passed_along(gradient, "pipe", -1)
    input_inverse = invert(input_factors[0])
    output_inverse = invert(output_factors[0])
    mixed = matmul(matmul(coupling_block, following), coupling_out.T)
    coupled = gradient - mixed
    scaled = matmul(matmul(input_inverse, coupled), output_inverse)
    carried = matmul(matmul(coupling_block.T, scaled), coupling_out)
    earlier = passed_along(carried, "pipe", 1)
    update = scaled - earlier
    return update[None]


def solution(mesh):
    in_specs = (
        P("pipe", "dp", None),
        P("pipe", "dp", None),
        P("pipe", "dp", None),
        P("pipe", None, None),
        P("pipe", "dp", None),
        P("pipe", None, None),
    )
    out_specs = P("pipe", "dp", None)
    return jax.shard_map(shards, mesh=mesh, in_specs=in_specs, out_specs=out_specs, check_vma=False)
```

profile of v0, /device:TPU:4, one launch (start us, length us, event | category | flops | bytes accessed | tf_op | source)
XLA Modules:
  0.0 83.5 jit_solution(5397005793444120427)
XLA Ops:
  6.5 0.7 all-gather.3.cloned.1.call-update
  7.3 2.1 %copy.7 = bf16[1,256,1024]{1,2,0:T(8,128)(2,1)} copy(bf16[1,256,1024]{2,1,0:T(8,128)(2,1)} %param.6) | data formatting | bytes 1048576 | tf_op args[0]
  9.4 5.0 %all-to-all-start = ((bf16[256,4,256]{0,2,1:T(8,128)(2,1)}), bf16[256,4,256]{0,2,1:T(8,128)(2,1)}, u32[]{:S(2)}, u32[]{:S(2)}) async-start(bf16[256,4,256]{0,2,1:T(8,128)(2,1)} %bitcast.3), calls=%async_computation | async-start | bytes 1048576 | tf_op jit(solution)/shard_map/all_to_all | solution.py:38
  14.7 0.6 reduce_max.18
  15.3 0.7 reduce_max.19
  18.2 1.8 %select_subtract_fusion.1 = f32[512,512]{0,1:T(8,128)S(1)} fusion(f32[1,512,512]{2,1,0:T(8,128)S(1)} %copy-done.1, f32[]{:T(128)S(6)} %divide.7), kind=kOutput, calls=%fused_computation.1 | convolution fusion | flops 1611923456 | bytes 2097156 | tf_op jit(solution)/shard_map/dot_general | solution.py:16
  20.0 1.3 %fusion.9 = f32[256,256]{0,1:T(8,128)} fusion(f32[256,256]{1,0:T(8,128)S(1)} %fusion.23, f32[1,256,256]{2,1,0:T(8,128)S(1)} %copy-done.3), kind=kOutput, calls=%fused_computation.10 | convolution fusion | flops 201523200 | bytes 786432 | tf_op jit(solution)/shard_map/dot_general | solution.py:16
  21.3 1.9 %fusion = f32[512,512]{1,0:T(8,128)S(1)} fusion(f32[512,512]{0,1:T(8,128)S(1)} %select_subtract_fusion.1, f32[]{:T(128)S(6)} %divide.7), kind=kOutput, calls=%fused_computation.2 | convolution fusion | flops 1611137024 | bytes 2097156 | tf_op jit(solution)/shard_map/dot_general | solution.py:16
  23.3 3.5 %select_subtract_fusion = f32[512,512]{0,1:T(8,128)S(1)} fusion(f32[512,512]{1,0:T(8,128)S(1)} %fusion, f32[1,512,512]{2,1,0:T(8,128)S(1)} %copy-done.2), kind=kOutput, calls=%fused_computation | convolution fusion | flops 1611399168 | bytes 3145728 | tf_op jit(solution)/shard_map/dot_general | solution.py:16
  26.7 12.9 %all-to-all-done = bf16[256,4,256]{0,2,1:T(8,128)(2,1)} async-done(((bf16[256,4,256]{0,2,1:T(8,128)(2,1)}), bf16[256,4,256]{0,2,1:T(8,128)(2,1)}, u32[]{:S(2)}, u32[]{:S(2)}) %all-to-all-start) | async-done | bytes 524320 | tf_op jit(solution)/shard_map/all_to_all | solution.py:38
  39.6 2.0 %copy.8 = bf16[4,256,256]{2,1,0:T(8,128)(2,1)} copy(bf16[4,256,256]{1,2,0:T(8,128)(2,1)} %bitcast.4) | data formatting | bytes 1048576 | tf_op jit(solution)/shard_map/all_to_all | solution.py:38
  41.7 4.4 %all-gather.3.cloned.1.call-done = bf16[1,1024,512]{2,1,0:T(8,128)(2,1)} async-done(((bf16[1,256,512]{2,1,0:T(8,128)(2,1)}), bf16[1,1024,512]{2,1,0:T(8,128)(2,1)}) %all-gather.3.cloned.1.call-update) | async-done | bytes 1048592 | tf_op jit(solution)/shard_map/all_gather | solution.py:39
  46.1 1.9 %fusion.17 = f32[256,512]{1,0:T(8,128)S(1)} fusion(bf16[1024,256]{1,0:T(8,128)(2,1)} %bitcast.67, bf16[1,1024,512]{2,1,0:T(8,128)(2,1)} %all-gather.3.cloned.1.call-done), kind=kOutput, calls=%fused_computation.20 | convolution fusion | flops 268435456 | bytes 2097152 | tf_op jit(solution)/shard_map/dot_general | solution.py:30
  48.0 3.1 %collective-permute-start = (f32[256,512]{1,0:T(8,128)S(1)}, f32[256,512]{1,0:T(8,128)S(1)}, u32[]{:S(2)}, u32[]{:S(2)}) collective-permute-start(f32[256,512]{1,0:T(8,128)S(1)} %fusion.17), channel_id=1, source_target_pairs={{4,0},{8,4},{12,8},{16,12},{20,16},{24,20},{28,24},{5,1},{9,5},{13... | collective-permute-start | bytes 1572872 | tf_op jit(solution)/shard_map/ppermute | solution.py:12
  51.6 1.9 %fusion.43 = f32[512,512]{1,0:T(8,128)S(1)} fusion(f32[512,512]{1,0:T(8,128)S(1)} %fusion, f32[512,512]{0,1:T(8,128)S(1)} %select_subtract_fusion), kind=kOutput, calls=%fused_computation.50 | convolution fusion | flops 1610612736 | bytes 3145728 | tf_op jit(solution)/shard_map/dot_general | solution.py:16
  53.4 4.2 %collective-permute-done = f32[256,512]{1,0:T(8,128)S(1)} collective-permute-done((f32[256,512]{1,0:T(8,128)S(1)}, f32[256,512]{1,0:T(8,128)S(1)}, u32[]{:S(2)}, u32[]{:S(2)}) %collective-permute-start) | collective-permute-done | bytes 524320 | tf_op jit(solution)/shard_map/ppermute | solution.py:12
  57.6 1.0 %fusion.28 = f32[512,256]{1,0:T(8,128)S(1)} fusion(f32[256,512]{1,0:T(8,128)S(1)} %collective-permute-done, f32[1,256,256]{2,1,0:T(8,128)S(1)} %copy-done.4), kind=kOutput, calls=%fused_computation.33 | convolution fusion | flops 402653184 | bytes 1310720 | tf_op jit(solution)/shard_map/dot_general | solution.py:16
  58.6 1.9 %convolution_subtract_fusion = f32[256,512]{1,0:T(8,128)S(1)} fusion(f32[256,512]{1,0:T(8,128)S(1)} %fusion.17, f32[512,256]{1,0:T(8,128)S(1)} %fusion.28, f32[1,512,512]{2,1,0:T(8,128)S(1)} %copy-done), kind=kOutput, calls=%fused_computation.8 | convolution fusion | flops 805437440 | bytes 2621440 | tf_op jit(solution)/shard_map/dot_general | solution.py:16
  61.1 1.1 %fusion.44 = f32[256,512]{1,0:T(8,128)S(1)} fusion(f32[256,512]{1,0:T(8,128)S(1)} %fusion.42, f32[512,512]{1,0:T(8,128)S(1)} %fusion.43), kind=kOutput, calls=%fused_computation.51 | convolution fusion | flops 805306368 | bytes 2097152 | tf_op jit(solution)/shard_map/dot_general | solution.py:16
  62.2 1.0 %fusion.26 = f32[512,256]{1,0:T(8,128)S(1)} fusion(f32[256,512]{1,0:T(8,128)S(1)} %fusion.44, f32[1,256,256]{2,1,0:T(8,128)S(1)} %copy-done.4), kind=kOutput, calls=%fused_computation.31 | convolution fusion | flops 402653184 | bytes 1310720 | tf_op jit(solution)/shard_map/dot_general | solution.py:16
  63.2 1.1 %fusion.14 = f32[256,512]{1,0:T(8,128)S(1)} fusion(f32[512,256]{1,0:T(8,128)S(1)} %fusion.26, f32[1,512,512]{2,1,0:T(8,128)S(1)} %copy-done), kind=kOutput, calls=%fused_computation.17 | convolution fusion | flops 805306368 | bytes 2097152 | tf_op jit(solution)/shard_map/dot_general | solution.py:16
  64.3 2.8 %collective-permute-start.1 = (f32[256,512]{1,0:T(8,128)S(1)}, f32[256,512]{1,0:T(8,128)S(1)}, u32[]{:S(2)}, u32[]{:S(2)}) collective-permute-start(f32[256,512]{1,0:T(8,128)S(1)} %fusion.14), channel_id=1, source_target_pairs={{0,4},{4,8},{8,12},{12,16},{16,20},{20,24},{24,28},{1,5},{5,9},{9,... | collective-permute-start | bytes 1572872 | tf_op jit(solution)/shard_map/ppermute | solution.py:12
  67.0 8.8 %collective-permute-done.1 = f32[256,512]{1,0:T(8,128)S(1)} collective-permute-done((f32[256,512]{1,0:T(8,128)S(1)}, f32[256,512]{1,0:T(8,128)S(1)}, u32[]{:S(2)}, u32[]{:S(2)}) %collective-permute-start.1) | collective-permute-done | bytes 524320 | tf_op jit(solution)/shard_map/ppermute | solution.py:12
  75.8 0.9 %subtract_bitcast_fusion = f32[1,256,512]{2,1,0:T(8,128)} fusion(f32[256,512]{1,0:T(8,128)S(1)} %fusion.44, f32[256,512]{1,0:T(8,128)S(1)} %collective-permute-done.1), kind=kLoop, calls=%fused_computation.23 | loop fusion | flops 131072 | bytes 1572864 | tf_op jit(solution)/shard_map/broadcast_in_dim | solution.py:51
  (19 shorter events, 2.2 us)
Async XLA Ops:
  6.5 52.1 %copy-start = (f32[1,512,512]{2,1,0:T(8,128)S(1)}, f32[1,512,512]{2,1,0:T(8,128)}, u32[]{:S(2)}) copy-start(f32[1,512,512]{2,1,0:T(8,128)} %param.11) | copy-start | bytes 3145732
  6.5 39.6 %all-gather.3.cloned.1.call-start = ((), (), s32[]{:S(2)}) async-start(), calls=%async_computation.1 | async-start | bytes 1310720 | tf_op jit(solution)/shard_map/all_gather | solution.py:39
  7.3 7.3 %copy-start.1 = (f32[1,512,512]{2,1,0:T(8,128)S(1)}, f32[1,512,512]{2,1,0:T(8,128)}, u32[]{:S(2)}) copy-start(f32[1,512,512]{2,1,0:T(8,128)} %param.9) | copy-start | bytes 3145732
  9.4 5.0 %copy-start.3 = (f32[1,256,256]{2,1,0:T(8,128)S(1)}, f32[1,256,256]{2,1,0:T(8,128)}, u32[]{:S(2)}) copy-start(f32[1,256,256]{2,1,0:T(8,128)} %param.8) | copy-start | bytes 786436
  9.4 30.2 %all-to-all-start = ((bf16[256,4,256]{0,2,1:T(8,128)(2,1)}), bf16[256,4,256]{0,2,1:T(8,128)(2,1)}, u32[]{:S(2)}, u32[]{:S(2)}) async-start(bf16[256,4,256]{0,2,1:T(8,128)(2,1)} %bitcast.3), calls=%async_computation | async-start | bytes 1048576 | tf_op jit(solution)/shard_map/all_to_all | solution.py:38
  21.3 1.9 %copy-start.2 = (f32[1,512,512]{2,1,0:T(8,128)S(1)}, f32[1,512,512]{2,1,0:T(8,128)}, u32[]{:S(2)}) copy-start(f32[1,512,512]{2,1,0:T(8,128)} %param.9) | copy-start | bytes 3145732
  46.1 5.0 %copy-start.5 = (f32[256,256]{0,1:T(8,128)S(1)}, f32[256,256]{0,1:T(8,128)}, u32[]{:S(2)}) copy-start(f32[256,256]{0,1:T(8,128)} %fusion.9) | copy-start | bytes 786436
  48.0 9.6 %collective-permute-start = (f32[256,512]{1,0:T(8,128)S(1)}, f32[256,512]{1,0:T(8,128)S(1)}, u32[]{:S(2)}, u32[]{:S(2)}) collective-permute-start(f32[256,512]{1,0:T(8,128)S(1)} %fusion.17), channel_id=1, source_target_pairs={{4,0},{8,4},{12,8},{16,12},{20,16},{24,20},{28,24},{5,1},{9,5},{13... | collective-permute-start | bytes 1572872 | tf_op jit(solution)/shard_map/ppermute | solution.py:12
  51.5 6.1 %copy-start.4 = (f32[1,256,256]{2,1,0:T(8,128)S(1)}, f32[1,256,256]{2,1,0:T(8,128)}, u32[]{:S(2)}) copy-start(f32[1,256,256]{2,1,0:T(8,128)} %param.10) | copy-start | bytes 786436
  64.3 11.6 %collective-permute-start.1 = (f32[256,512]{1,0:T(8,128)S(1)}, f32[256,512]{1,0:T(8,128)S(1)}, u32[]{:S(2)}, u32[]{:S(2)}) collective-permute-start(f32[256,512]{1,0:T(8,128)S(1)} %fusion.14), channel_id=1, source_target_pairs={{0,4},{4,8},{8,12},{12,16},{16,20},{20,24},{24,28},{1,5},{5,9},{9,... | collective-permute-start | bytes 1572872 | tf_op jit(solution)/shard_map/ppermute | solution.py:12
Sparse Core Ops, SparseCore 0:
  8.9 37.1 all-gather.2
where the time goes:
time: 83.9 us; the launch traced here: 83.5 us
  waiting for transfers between devices  31 us (37%)
  matrix products  20.1 us (24%)
  between operations  14.9 us (18%)
  starting transfers between devices  10.9 us (13%)
  local copies, waits for them, and re-layouts  4.2 us (5%)
  other arithmetic  2.45 us (3%)
    dot_general x14, matrix products, matmul(): return jnp.matmul(left, right, precision=lax.Precision.HIGHEST)  18.2 us
    ppermute x2, waiting for transfers between devices, passed_along(): lax.ppermute(value, axis, [(source, source + steps) for source in range(f...  13 us
    all_to_all x1, waiting for transfers between devices, shards(): lax.all_to_all(panel_rows, 'dp', split_axis=1, concat_axis=0, tiled=True)  12.9 us
    ppermute x2, starting transfers between devices, passed_along(): lax.ppermute(value, axis, [(source, source + steps) for source in range(f...  5.9 us
    all_to_all x1, starting transfers between devices, shards(): lax.all_to_all(panel_rows, 'dp', split_axis=1, concat_axis=0, tiled=True)  5 us
    all_gather x1, waiting for transfers between devices, shards(): lax.all_gather(cotangent_block, 'dp', axis=0, tiled=True)  4.43 us
    unnamed x13, local copies, waits for them, and re-layouts  2.16 us
    all_to_all x1, local copies, waits for them, and re-layouts, shards(): lax.all_to_all(panel_rows, 'dp', split_axis=1, concat_axis=0, tiled=True)  2.04 us
  transfers between devices with their start and end apart: 4, of which 4 were waited for; matrix products, arithmetic and copies ran while one was open for 21% of the time, Pallas kernels for 0%

commit v1 on v0

v1 whole, which is shorter than its diff:
```python
import functools

import jax
import jax.numpy as jnp
from jax import lax
from jax.experimental import pallas as pl
from jax.experimental.pallas import tpu as pltpu
from jax.sharding import PartitionSpec as P

MESH = pl.DeviceIdType.MESH
F32 = jnp.float32
BF16 = jnp.bfloat16
WIDTH = 128


def split(value):
    high = value.astype(BF16)
    return high, (value - high.astype(F32)).astype(BF16)


def dot(left, right):
    return jnp.dot(left, right, preferred_element_type=F32)


def dot3(left, right):
    (lh, ll), (rh, rl) = left, right
    return dot(lh, rh) + (dot(lh, rl) + dot(ll, rh))


def invert(factor):
    order = factor.shape[-1]
    bound = jnp.max(jnp.sum(jnp.abs(factor), axis=1, keepdims=True))
    scaled = factor / bound
    rows = lax.broadcasted_iota(jnp.int32, (order, order), 0)
    cols = lax.broadcasted_iota(jnp.int32, (order, order), 1)
    four = jnp.where(rows == cols, jnp.float32(4.0), jnp.float32(0.0))
    parts = split(scaled)
    square = dot3(parts, parts)
    cubic = dot3(split(square), split(four - scaled))
    return (four - 6.0 * scaled + cubic) / bound


def kernel(
    layers, n,
    x_ref, c_ref, a_ref, b_ref, p_ref, q_ref,
    out_ref,
    xcols, xt, call, a_v, b_v, p_v, q_v,
    ia, ib, ph, pt, qh, qt,
    grad, follow, mixed, scaled, carried, earlier,
    local_sem, xsend, xrecv, csend, crecv, gsend, grecv, ksend, krecv,
):
    layer, me = lax.axis_index("pipe"), lax.axis_index("dp")
    tokens, block = xcols.shape[1], xcols.shape[2]
    outc = grad.shape[1]
    width = min(WIDTH, outc)
    chunks = outc // width
    has_next, has_prev = layer < layers - 1, layer > 0

    def span(index):
        return pl.ds(index * width, width)

    def columns(index):
        return pl.ds(pl.multiple_of(index * block, block), block)

    locals_ = [
        pltpu.make_async_copy(src, dst, local_sem.at[i])
        for i, (src, dst) in enumerate([
            (b_ref.at[0], b_v), (a_ref.at[0], a_v), (p_ref.at[0], p_v), (q_ref.at[0], q_v),
            (x_ref.at[0, :, columns(me)], xcols.at[me]), (c_ref.at[0], call.at[me]),
        ])
    ]

    barrier = pltpu.get_barrier_semaphore()
    for d in range(1, n):
        pl.semaphore_signal(barrier, inc=1, device_id=(layer, lax.rem(me + d, n)), device_id_type=MESH)

    @pl.when(has_prev)
    def _():
        pl.semaphore_signal(barrier, inc=1, device_id=(layer - 1, me), device_id_type=MESH)

    @pl.when(has_next)
    def _():
        pl.semaphore_signal(barrier, inc=1, device_id=(layer + 1, me), device_id_type=MESH)

    for copy in locals_:
        copy.start()
    pl.semaphore_wait(barrier, n - 1 + has_prev.astype(jnp.int32) + has_next.astype(jnp.int32))

    def x_copy(target):
        return pltpu.make_async_remote_copy(
            src_ref=x_ref.at[0, :, columns(target)], dst_ref=xcols.at[me],
            send_sem=xsend.at[target], recv_sem=xrecv.at[me],
            device_id=(layer, target), device_id_type=MESH)

    def x_arrival(source):
        return pltpu.make_async_remote_copy(
            src_ref=xcols.at[source], dst_ref=xcols.at[source],
            send_sem=xsend.at[source], recv_sem=xrecv.at[source],
            device_id=(layer, source), device_id_type=MESH)

    for d in range(n - 1, 0, -1):
        for target in (me + d, me - d):
            @pl.when((target >= 0) & (target < n))
            def _(target=target):
                x_copy(target).start()

    def c_copy(source, chunk, step, own=False):
        block_ref = call.at[source, :, span(chunk)]
        return pltpu.make_async_remote_copy(
            src_ref=c_ref.at[0, :, span(chunk)] if own else block_ref, dst_ref=block_ref,
            send_sem=csend.at[(step + 1) // 2, source, chunk], recv_sem=crecv.at[source, chunk],
            device_id=(layer, me + step), device_id_type=MESH)

    def can_go(step):
        return me < n - 1 if step > 0 else me > 0

    def send_own(chunk):
        for step in (1, -1):
            @pl.when(can_go(step))
            def _(step=step):
                c_copy(me, chunk, step, True).start()

    def relay(chunk):
        for d in range(1, n):
            for step in (1, -1):
                source = me - step * d

                @pl.when((source >= 0) & (source < n))
                def _(source=source, step=step):
                    c_copy(source, chunk, -step).wait_recv()

                    @pl.when(can_go(step))
                    def _():
                        c_copy(source, chunk, step).start()

    def g_copy(chunk):
        return pltpu.make_async_remote_copy(
            src_ref=grad.at[:, span(chunk)], dst_ref=follow.at[:, span(chunk)],
            send_sem=gsend.at[chunk], recv_sem=grecv.at[chunk],
            device_id=(layer - 1, me), device_id_type=MESH)

    def k_copy(chunk):
        return pltpu.make_async_remote_copy(
            src_ref=carried.at[:, span(chunk)], dst_ref=earlier.at[:, span(chunk)],
            send_sem=ksend.at[chunk], recv_sem=krecv.at[chunk],
            device_id=(layer + 1, me), device_id_type=MESH)

    def put(ref, value):
        ref[0], ref[1] = split(value)

    def both(ref, *index):
        return ref[(0, *index)], ref[(1, *index)]

    send_own(0)

    for copy in locals_:
        copy.wait()
    put(ib, invert(b_v[...]))
    put(ia, invert(a_v[...]))
    put(ph, p_v[...])
    put(pt, p_v[...].T)
    put(qh, q_v[...])
    put(qt, q_v[...].T)
    mixed[...] = jnp.zeros_like(mixed)

    @pl.when(jnp.logical_not(has_next))
    def _():
        follow[...] = jnp.zeros_like(follow)

    @pl.when(jnp.logical_not(has_prev))
    def _():
        earlier[...] = jnp.zeros_like(earlier)

    for source in range(n):
        @pl.when(source != me)
        def _(source=source):
            x_arrival(source).wait_recv()

        xt[:, source * tokens:(source + 1) * tokens] = xcols[source].T

    def mix(chunk):
        @pl.when(has_next)
        def _():
            g_copy(chunk).wait_recv()

        part = dot3(both(ph), split(follow[:, chunk * width:(chunk + 1) * width]))
        mixed[...] += dot3(split(part), both(qt, slice(chunk * width, (chunk + 1) * width)))

    for chunk in range(chunks):
        if chunk + 1 < chunks:
            send_own(chunk + 1)
        relay(chunk)
        right = call[:, :, chunk * width:(chunk + 1) * width].reshape(n * tokens, width)
        grad[:, chunk * width:(chunk + 1) * width] = dot(xt[...], right)

        @pl.when(has_prev)
        def _(chunk=chunk):
            g_copy(chunk).start()

        if chunk > 0:
            mix(chunk - 1)
    mix(chunks - 1)

    coupled = grad[...] - mixed[...]
    half = dot3(both(ia), split(coupled))
    scaled[...] = dot3(split(half), both(ib))
    half = split(dot3(both(pt), split(scaled[...])))
    for chunk in range(chunks):
        carried[:, chunk * width:(chunk + 1) * width] = dot3(
            half, both(qh, slice(None), slice(chunk * width, (chunk + 1) * width)))

        @pl.when(has_next)
        def _(chunk=chunk):
            k_copy(chunk).start()

    for chunk in range(chunks):
        @pl.when(has_prev)
        def _(chunk=chunk):
            k_copy(chunk).wait_recv()

        part = slice(chunk * width, (chunk + 1) * width)
        out_ref[:, part] = scaled[:, part] - earlier[:, part]

    for d in range(n - 1, 0, -1):
        for target in (me + d, me - d):
            @pl.when((target >= 0) & (target < n))
            def _(target=target):
                x_copy(target).wait_send()
    for chunk in range(chunks):
        for step in (1, -1):
            for d in range(n):
                source = me - step * d

                @pl.when((source >= 0) & (source < n) & can_go(step))
                def _(source=source, step=step, chunk=chunk, d=d):
                    c_copy(source, chunk, step, d == 0).wait_send()

        @pl.when(has_prev)
        def _(chunk=chunk):
            g_copy(chunk).wait_send()

        @pl.when(has_next)
        def _(chunk=chunk):
            k_copy(chunk).wait_send()


def shards(layers, n, inputs, cotangents, input_factors, output_factors, input_coupling, output_coupling):
    tokens = inputs.shape[1]
    block = input_factors.shape[2]
    outc = cotangents.shape[2]
    chunks = outc // min(WIDTH, outc)
    dma = pltpu.SemaphoreType.DMA
    panel = pltpu.VMEM((block, outc), F32)
    out = pl.pallas_call(
        functools.partial(kernel, layers, n),
        out_shape=jax.ShapeDtypeStruct((block, outc), F32),
        in_specs=[pl.BlockSpec(memory_space=pl.ANY)] * 6,
        out_specs=pl.BlockSpec(memory_space=pltpu.VMEM),
        scratch_shapes=[
            pltpu.VMEM((n, tokens, block), BF16),
            pltpu.VMEM((block, n * tokens), BF16),
            pltpu.VMEM((n, tokens, outc), BF16),
            pltpu.VMEM((block, block), F32),
            pltpu.VMEM((outc, outc), F32),
            pltpu.VMEM((block, block), F32),
            pltpu.VMEM((outc, outc), F32),
            pltpu.VMEM((2, block, block), BF16),
            pltpu.VMEM((2, outc, outc), BF16),
            pltpu.VMEM((2, block, block), BF16),
            pltpu.VMEM((2, block, block), BF16),
            pltpu.VMEM((2, outc, outc), BF16),
            pltpu.VMEM((2, outc, outc), BF16),
            panel, panel, panel, panel, panel, panel,
            dma((6,)),
            dma((n,)), dma((n,)),
            dma((2, n, chunks)), dma((n, chunks)),
            dma((chunks,)), dma((chunks,)), dma((chunks,)), dma((chunks,)),
        ],
        compiler_params=pltpu.CompilerParams(
            collective_id=0, has_side_effects=True, vmem_limit_bytes=60 * 1024 * 1024),
    )(inputs, cotangents, input_factors, output_factors, input_coupling, output_coupling)
    return out[None]


def solution(mesh):
    in_specs = (
        P("pipe", "dp", None),
        P("pipe", "dp", None),
        P("pipe", "dp", None),
        P("pipe", None, None),
        P("pipe", "dp", None),
        P("pipe", None, None),
    )
    body = functools.partial(shards, mesh.shape["pipe"], mesh.shape["dp"])
    return jax.shard_map(body, mesh=mesh, in_specs=in_specs, out_specs=P("pipe", "dp", None), check_vma=False)
```

time: 83.9 us -> 58.5 us (0.70)
  Pallas kernels: 0 us -> 56.4 us
  waiting for transfers between devices: 31 us -> 0 us
  matrix products: 20.1 us -> 0 us
  between operations: 14.9 us -> 0.01 us
  starting transfers between devices: 10.9 us -> 0 us
  other arithmetic: 2.45 us -> 0 us
  local copies, waits for them, and re-layouts: 4.2 us -> 1.87 us
    pallas_call x0 -> x1, Pallas kernels: none -> 56.4 us  [shards(): pl.pallas_call(functools.partial(kernel, layers, n), out_shape=jax.ShapeD...]
    dot_general x15 -> x0, matrix products: 20.1 us -> none  [the longest x14 18.2 us: matmul(): return jnp.matmul(left, right, precision=lax.Precision.HIGHEST)]
    ppermute x2 -> x0, waiting for transfers between devices: 13 us -> none  [passed_along(): lax.ppermute(value, axis, [(source, source + steps) for source in range(f...]
    all_to_all x1 -> x0, waiting for transfers between devices: 12.9 us -> none  [shards(): lax.all_to_all(panel_rows, 'dp', split_axis=1, concat_axis=0, tiled=True)]
    ppermute x2 -> x0, starting transfers between devices: 5.9 us -> none  [passed_along(): lax.ppermute(value, axis, [(source, source + steps) for source in range(f...]
    all_to_all x1 -> x0, starting transfers between devices: 5 us -> none  [shards(): lax.all_to_all(panel_rows, 'dp', split_axis=1, concat_axis=0, tiled=True)]
    all_gather x1 -> x0, waiting for transfers between devices: 4.43 us -> none  [shards(): lax.all_gather(cotangent_block, 'dp', axis=0, tiled=True)]
    all_to_all x1 -> x0, local copies, waits for them, and re-layouts: 2.04 us -> none  [shards(): lax.all_to_all(panel_rows, 'dp', split_axis=1, concat_axis=0, tiled=True)]
  transfers between devices with their start and end apart: 4 -> 0, of which waited for: 4 -> 0; matrix products, arithmetic and copies ran while one was open for 21% -> 0% of each run, Pallas kernels for 0% -> 0%
where the time goes in v1:
time: 58.5 us; the launch traced here: 58.3 us
  Pallas kernels  56.4 us (96%)
  local copies, waits for them, and re-layouts  1.87 us (3%)
    pallas_call x1, Pallas kernels, shards(): pl.pallas_call(functools.partial(kernel, layers, n), out_shape=jax.ShapeD...  56.4 us
    unnamed x1, local copies, waits for them, and re-layouts  1.87 us

profile of v1, /device:TPU:4, one launch (start us, length us, event | category | flops | bytes accessed | tf_op | source)
XLA Modules:
  0.0 58.3 jit_solution(10796152945479215379)
XLA Ops:
  0.0 56.4 %shard_map.64 = f32[256,512]{1,0:T(8,128)} custom-call(bf16[1,256,1024]{2,1,0:T(8,128)(2,1)} %x_ref.1, bf16[1,256,512]{2,1,0:T(8,128)(2,1)} %c_ref.1, f32[1,256,256]{2,1,0:T(8,128)} %a_ref.1, f32[1,512,512]{2,1,0:T(8,128)} %b_ref.1, f32[1,256,256]{2,1,0:T(8,128)} %p_ref.1, f32[1,512,512]{2,1,0:T(8,128)} %q_ref.1), custom_call_target="tpu_custom_call" | custom-call | tf_op jit(solution)/shard_map/pallas_call | solution.py:254
  56.4 1.9 %copy.8 = f32[1,256,512]{2,1,0:T(8,128)} copy(f32[1,256,512]{2,1,0:T(8,128)} %bitcast.1) | data formatting | bytes 1048576

commit v2 on v1

--- a/solution.py
+++ b/solution.py
@@ -11,6 +11,7 @@
 F32 = jnp.float32
 BF16 = jnp.bfloat16
 WIDTH = 128
+LOOKAHEAD = 2
 
 
 def split(value):
@@ -43,10 +44,10 @@
 def kernel(
     layers, n,
     x_ref, c_ref, a_ref, b_ref, p_ref, q_ref,
-    out_ref,
+    scaled_ref, earlier_ref,
     xcols, xt, call, a_v, b_v, p_v, q_v,
-    ia, ib, ph, pt, qh, qt,
-    grad, follow, mixed, scaled, carried, earlier,
+    ia, ib, ph, pa, bq, qt,
+    grad, follow, mixed, scaled, carried,
     local_sem, xsend, xrecv, csend, crecv, gsend, grecv, ksend, krecv,
 ):
     layer, me = lax.axis_index("pipe"), lax.axis_index("dp")
@@ -120,13 +121,16 @@
             def _(step=step):
                 c_copy(me, chunk, step, True).start()
 
-    def relay(chunk):
+    def relay(turn):
         for d in range(1, n):
+            chunk = turn - (d - 1)
+            if not 0 <= chunk < chunks:
+                continue
             for step in (1, -1):
                 source = me - step * d
 
                 @pl.when((source >= 0) & (source < n))
-                def _(source=source, step=step):
+                def _(source=source, step=step, chunk=chunk):
                     c_copy(source, chunk, -step).wait_recv()
 
                     @pl.when(can_go(step))
@@ -141,7 +145,7 @@
 
     def k_copy(chunk):
         return pltpu.make_async_remote_copy(
-            src_ref=carried.at[:, span(chunk)], dst_ref=earlier.at[:, span(chunk)],
+            src_ref=carried.at[:, span(chunk)], dst_ref=earlier_ref.at[:, span(chunk)],
             send_sem=ksend.at[chunk], recv_sem=krecv.at[chunk],
             device_id=(layer + 1, me), device_id_type=MESH)
 
@@ -151,25 +155,30 @@
     def both(ref, *index):
         return ref[(0, *index)], ref[(1, *index)]
 
-    send_own(0)
+    for chunk in range(min(LOOKAHEAD, chunks)):
+        send_own(chunk)
 
     for copy in locals_:
         copy.wait()
+    carried[...] = jnp.zeros_like(carried)
     put(ib, invert(b_v[...]))
     put(ia, invert(a_v[...]))
     put(ph, p_v[...])
-    put(pt, p_v[...].T)
-    put(qh, q_v[...])
     put(qt, q_v[...].T)
+    put(pa, dot3(split(p_v[...].T), both(ia)))
+    put(bq, dot3(both(ib), split(q_v[...])))
+
+    @pl.when(jnp.logical_not(has_prev))
+    def _():
+        blank = pltpu.make_async_copy(carried, earlier_ref, local_sem.at[0])
+        blank.start()
+        blank.wait()
+
     mixed[...] = jnp.zeros_like(mixed)
 
     @pl.when(jnp.logical_not(has_next))
     def _():
         follow[...] = jnp.zeros_like(follow)
-
-    @pl.when(jnp.logical_not(has_prev))
-    def _():
-        earlier[...] = jnp.zeros_like(earlier)
 
     for source in range(n):
         @pl.when(source != me)
@@ -186,10 +195,13 @@
         part = dot3(both(ph), split(follow[:, chunk * width:(chunk + 1) * width]))
         mixed[...] += dot3(split(part), both(qt, slice(chunk * width, (chunk + 1) * width)))
 
-    for chunk in range(chunks):
-        if chunk + 1 < chunks:
-            send_own(chunk + 1)
-        relay(chunk)
+    for turn in range(chunks + n - 2):
+        if turn + LOOKAHEAD < chunks:
+            send_own(turn + LOOKAHEAD)
+        relay(turn)
+        chunk = turn - (n - 2)
+        if chunk < 0:
+            continue
         right = call[:, :, chunk * width:(chunk + 1) * width].reshape(n * tokens, width)
         grad[:, chunk * width:(chunk + 1) * width] = dot(xt[...], right)
 
@@ -201,25 +213,25 @@
             mix(chunk - 1)
     mix(chunks - 1)
 
-    coupled = grad[...] - mixed[...]
-    half = dot3(both(ia), split(coupled))
-    scaled[...] = dot3(split(half), both(ib))
-    half = split(dot3(both(pt), split(scaled[...])))
+    coupled = split(grad[...] - mixed[...])
+    half = split(dot3(both(pa), coupled))
     for chunk in range(chunks):
         carried[:, chunk * width:(chunk + 1) * width] = dot3(
-            half, both(qh, slice(None), slice(chunk * width, (chunk + 1) * width)))
+            half, both(bq, slice(None), slice(chunk * width, (chunk + 1) * width)))
 
         @pl.when(has_next)
         def _(chunk=chunk):
             k_copy(chunk).start()
 
+    scaled[...] = dot3(split(dot3(both(ia), coupled)), both(ib))
+    result = pltpu.make_async_copy(scaled, scaled_ref, local_sem.at[0])
+    result.start()
     for chunk in range(chunks):
         @pl.when(has_prev)
         def _(chunk=chunk):
             k_copy(chunk).wait_recv()
 
-        part = slice(chunk * width, (chunk + 1) * width)
-        out_ref[:, part] = scaled[:, part] - earlier[:, part]
+    result.wait()
 
     for d in range(n - 1, 0, -1):
         for target in (me + d, me - d):
@@ -251,11 +263,11 @@
     chunks = outc // min(WIDTH, outc)
     dma = pltpu.SemaphoreType.DMA
     panel = pltpu.VMEM((block, outc), F32)
-    out = pl.pallas_call(
+    scaled, earlier = pl.pallas_call(
         functools.partial(kernel, layers, n),
-        out_shape=jax.ShapeDtypeStruct((block, outc), F32),
+        out_shape=[jax.ShapeDtypeStruct((block, outc), F32)] * 2,
         in_specs=[pl.BlockSpec(memory_space=pl.ANY)] * 6,
-        out_specs=pl.BlockSpec(memory_space=pltpu.VMEM),
+        out_specs=[pl.BlockSpec(memory_space=pl.ANY)] * 2,
         scratch_shapes=[
             pltpu.VMEM((n, tokens, block), BF16),
             pltpu.VMEM((block, n * tokens), BF16),
@@ -270,7 +282,7 @@
             pltpu.VMEM((2, block, block), BF16),
             pltpu.VMEM((2, outc, outc), BF16),
             pltpu.VMEM((2, outc, outc), BF16),
-            panel, panel, panel, panel, panel, panel,
+            panel, panel, panel, panel, panel,
             dma((6,)),
             dma((n,)), dma((n,)),
             dma((2, n, chunks)), dma((n, chunks)),
@@ -279,7 +291,7 @@
         compiler_params=pltpu.CompilerParams(
             collective_id=0, has_side_effects=True, vmem_limit_bytes=60 * 1024 * 1024),
     )(inputs, cotangents, input_factors, output_factors, input_coupling, output_coupling)
-    return out[None]
+    return (scaled - earlier)[None]
 
 
 def solution(mesh):

time: 58.5 us -> 49.1 us (0.84)
  Pallas kernels: 56.4 us -> 46.9 us
  other arithmetic: 0 us -> 2.07 us
  local copies, waits for them, and re-layouts: 1.87 us -> 0 us
    pallas_call x1, Pallas kernels: 56.4 us -> 46.9 us  [shards(): pl.pallas_call(functools.partial(kernel, layers, n), out_shape=[jax.Shape...]
    broadcast_in_dim x0 -> x1, other arithmetic: none -> 2.07 us  [shards(): return (scaled - earlier)[None]]
    unnamed x1 -> x0, local copies, waits for them, and re-layouts: 1.87 us -> none
where the time goes in v2:
time: 49.1 us; the launch traced here: 49 us
  Pallas kernels  46.9 us (96%)
  other arithmetic  2.07 us (4%)
    pallas_call x1, Pallas kernels, shards(): pl.pallas_call(functools.partial(kernel, layers, n), out_shape=[jax.Shape...  46.9 us
    broadcast_in_dim x1, other arithmetic, shards(): return (scaled - earlier)[None]  2.07 us

profile of v2, /device:TPU:4, one launch (start us, length us, event | category | flops | bytes accessed | tf_op | source)
XLA Modules:
  0.0 49.0 jit_solution(5238908385482573285)
XLA Ops:
  0.0 46.9 %shard_map.64 = (f32[256,512]{1,0:T(8,128)}, f32[256,512]{1,0:T(8,128)}) custom-call(bf16[1,256,1024]{2,1,0:T(8,128)(2,1)} %x_ref.1, bf16[1,256,512]{2,1,0:T(8,128)(2,1)} %c_ref.1, f32[1,256,256]{2,1,0:T(8,128)} %a_ref.1, f32[1,512,512]{2,1,0:T(8,128)} %b_ref.1, f32[1,256,256]{2,1,0:T(8,128)} %p_ref.1, f32[1,512,512]{2,1,0:T(8,128)} %q_ref.1), custom_call_target="tpu_custom_call" | custom-call | tf_op jit(solution)/shard_map/pallas_call | solution.py:266
  46.9 2.1 %subtract_bitcast_fusion = f32[1,256,512]{2,1,0:T(8,128)} fusion(f32[256,512]{1,0:T(8,128)} %get-tuple-element.7, f32[256,512]{1,0:T(8,128)} %get-tuple-element.8), kind=kLoop, calls=%fused_computation | loop fusion | flops 131072 | bytes 1572864 | tf_op jit(solution)/shard_map/broadcast_in_dim | solution.py:294

commit v3 on v2

--- a/solution.py
+++ b/solution.py
@@ -11,6 +11,7 @@
 F32 = jnp.float32
 BF16 = jnp.bfloat16
 WIDTH = 128
+VMEM = 67043328
 LOOKAHEAD = 2
 
 
@@ -47,7 +48,7 @@
     scaled_ref, earlier_ref,
     xcols, xt, call, a_v, b_v, p_v, q_v,
     ia, ib, ph, pa, bq, qt,
-    grad, follow, mixed, scaled, carried,
+    grad, follow, mixed, carried,
     local_sem, xsend, xrecv, csend, crecv, gsend, grecv, ksend, krecv,
 ):
     layer, me = lax.axis_index("pipe"), lax.axis_index("dp")
@@ -160,7 +161,6 @@
 
     for copy in locals_:
         copy.wait()
-    carried[...] = jnp.zeros_like(carried)
     put(ib, invert(b_v[...]))
     put(ia, invert(a_v[...]))
     put(ph, p_v[...])
@@ -170,9 +170,7 @@
 
     @pl.when(jnp.logical_not(has_prev))
     def _():
-        blank = pltpu.make_async_copy(carried, earlier_ref, local_sem.at[0])
-        blank.start()
-        blank.wait()
+        earlier_ref[...] = jnp.zeros_like(earlier_ref)
 
     mixed[...] = jnp.zeros_like(mixed)
 
@@ -223,15 +221,11 @@
         def _(chunk=chunk):
             k_copy(chunk).start()
 
-    scaled[...] = dot3(split(dot3(both(ia), coupled)), both(ib))
-    result = pltpu.make_async_copy(scaled, scaled_ref, local_sem.at[0])
-    result.start()
+    scaled_ref[...] = dot3(split(dot3(both(ia), coupled)), both(ib))
     for chunk in range(chunks):
         @pl.when(has_prev)
         def _(chunk=chunk):
             k_copy(chunk).wait_recv()
-
-    result.wait()
 
     for d in range(n - 1, 0, -1):
         for target in (me + d, me - d):
@@ -265,9 +259,9 @@
     panel = pltpu.VMEM((block, outc), F32)
     scaled, earlier = pl.pallas_call(
         functools.partial(kernel, layers, n),
-        out_shape=[jax.ShapeDtypeStruct((block, outc), F32)] * 2,
+        out_shape=[pltpu.VMEM((block, outc), F32)] * 2,
         in_specs=[pl.BlockSpec(memory_space=pl.ANY)] * 6,
-        out_specs=[pl.BlockSpec(memory_space=pl.ANY)] * 2,
+        out_specs=[pl.BlockSpec(memory_space=pltpu.VMEM)] * 2,
         scratch_shapes=[
             pltpu.VMEM((n, tokens, block), BF16),
             pltpu.VMEM((block, n * tokens), BF16),
@@ -282,14 +276,14 @@
             pltpu.VMEM((2, block, block), BF16),
             pltpu.VMEM((2, outc, outc), BF16),
             pltpu.VMEM((2, outc, outc), BF16),
-            panel, panel, panel, panel, panel,
+            panel, panel, panel, panel,
             dma((6,)),
             dma((n,)), dma((n,)),
             dma((2, n, chunks)), dma((n, chunks)),
             dma((chunks,)), dma((chunks,)), dma((chunks,)), dma((chunks,)),
         ],
         compiler_params=pltpu.CompilerParams(
-            collective_id=0, has_side_effects=True, vmem_limit_bytes=60 * 1024 * 1024),
+            collective_id=0, has_side_effects=True, vmem_limit_bytes=VMEM - 8 * block * outc - 65536),
     )(inputs, cotangents, input_factors, output_factors, input_coupling, output_coupling)
     return (scaled - earlier)[None]
 

time: 49.1 us -> 47.8 us (0.974)
  other arithmetic: 2.07 us -> 0.87 us
    broadcast_in_dim x1, other arithmetic: 2.07 us -> 0.87 us  [shards(): return (scaled - earlier)[None]]
where the time goes in v3:
time: 47.8 us; the launch traced here: 47.7 us
  Pallas kernels  46.8 us (98%)
  other arithmetic  0.87 us (2%)
    pallas_call x1, Pallas kernels, shards(): pl.pallas_call(functools.partial(kernel, layers, n), out_shape=[pltpu.VME...  46.8 us

profile of v3, /device:TPU:4, one launch (start us, length us, event | category | flops | bytes accessed | tf_op | source)
XLA Modules:
  0.0 47.7 jit_solution(3706014406188733764)
XLA Ops:
  0.0 46.8 %shard_map.64 = (f32[256,512]{1,0:T(8,128)S(1)}, f32[256,512]{1,0:T(8,128)S(1)}) custom-call(bf16[1,256,1024]{2,1,0:T(8,128)(2,1)} %x_ref.1, bf16[1,256,512]{2,1,0:T(8,128)(2,1)} %c_ref.1, f32[1,256,256]{2,1,0:T(8,128)} %a_ref.1, f32[1,512,512]{2,1,0:T(8,128)} %b_ref.1, f32[1,256,256]{2,1,0:T(8,128)} %p_ref.1, f32[1,512,512]{2,1,0:T(8,128)} %q_ref.1), custom_call_target="tpu_custom_call" | custom-call | tf_op jit(solution)/shard_map/pallas_call | solution.py:260
  46.8 0.9 %subtract_bitcast_fusion = f32[1,256,512]{2,1,0:T(8,128)} fusion(f32[256,512]{1,0:T(8,128)S(1)} %get-tuple-element.7, f32[256,512]{1,0:T(8,128)S(1)} %get-tuple-element.8), kind=kLoop, calls=%fused_computation | loop fusion | flops 131072 | bytes 1572864 | tf_op jit(solution)/shard_map/broadcast_in_dim | solution.py:288

commit v4 on v2

--- a/solution.py
+++ b/solution.py
@@ -11,6 +11,7 @@
 F32 = jnp.float32
 BF16 = jnp.bfloat16
 WIDTH = 128
+VMEM = 67043328
 LOOKAHEAD = 2
 
 
@@ -46,7 +47,7 @@
     x_ref, c_ref, a_ref, b_ref, p_ref, q_ref,
     scaled_ref, earlier_ref,
     xcols, xt, call, a_v, b_v, p_v, q_v,
-    ia, ib, ph, pa, bq, qt,
+    ia, ib, ph, pa, vp, bq, qt, qw,
     grad, follow, mixed, scaled, carried,
     local_sem, xsend, xrecv, csend, crecv, gsend, grecv, ksend, krecv,
 ):
@@ -164,9 +165,11 @@
     put(ib, invert(b_v[...]))
     put(ia, invert(a_v[...]))
     put(ph, p_v[...])
+    put(pa, dot3(split(p_v[...].T), both(ia)))
+    put(vp, dot3(both(pa), both(ph)))
     put(qt, q_v[...].T)
-    put(pa, dot3(split(p_v[...].T), both(ia)))
     put(bq, dot3(both(ib), split(q_v[...])))
+    put(qw, dot3(both(qt), both(bq)))
 
     @pl.when(jnp.logical_not(has_prev))
     def _():
@@ -187,42 +190,60 @@
 
         xt[:, source * tokens:(source + 1) * tokens] = xcols[source].T
 
-    def mix(chunk):
+    def mixed_in(chunk, next_parts):
+        part = slice(chunk * width, (chunk + 1) * width)
+        mixed[...] += dot3(split(dot3(both(ph), next_parts)), both(qt, part))
+
+    def arrived(chunk):
         @pl.when(has_next)
         def _():
             g_copy(chunk).wait_recv()
 
-        part = dot3(both(ph), split(follow[:, chunk * width:(chunk + 1) * width]))
-        mixed[...] += dot3(split(part), both(qt, slice(chunk * width, (chunk + 1) * width)))
-
+        return split(follow[:, chunk * width:(chunk + 1) * width])
+
+    def rows_of(ref, chunk):
+        return both(ref, slice(chunk * width, (chunk + 1) * width))
+
+    waiting = []
     for turn in range(chunks + n - 2):
         if turn + LOOKAHEAD < chunks:
             send_own(turn + LOOKAHEAD)
         relay(turn)
         chunk = turn - (n - 2)
         if chunk < 0:
+            if waiting:
+                waiting.pop(0)()
             continue
-        right = call[:, :, chunk * width:(chunk + 1) * width].reshape(n * tokens, width)
-        grad[:, chunk * width:(chunk + 1) * width] = dot(xt[...], right)
+        part = slice(chunk * width, (chunk + 1) * width)
+        right = call[:, :, part].reshape(n * tokens, width)
+        grad[:, part] = dot(xt[...], right)
 
         @pl.when(has_prev)
         def _(chunk=chunk):
             g_copy(chunk).start()
 
+        while waiting:
+            waiting.pop(0)()
+        carried[...] += dot3(split(dot3(both(pa), split(grad[:, part]))), rows_of(bq, chunk))
         if chunk > 0:
-            mix(chunk - 1)
-    mix(chunks - 1)
-
+            after = arrived(chunk - 1)
+            mixed_in(chunk - 1, after)
+            carried[...] -= dot3(split(dot3(both(vp), after)), rows_of(qw, chunk - 1))
+
+    last = chunks - 1
+    after = arrived(last)
+    half = split(dot3(both(vp), after))
+    rows = slice(last * width, (last + 1) * width)
+    for chunk in range(chunks):
+        part = slice(chunk * width, (chunk + 1) * width)
+        carried[:, part] -= dot3(half, both(qw, rows, part))
+
+        @pl.when(has_next)
+        def _(chunk=chunk):
+            k_copy(chunk).start()
+
+    mixed_in(last, after)
     coupled = split(grad[...] - mixed[...])
-    half = split(dot3(both(pa), coupled))
-    for chunk in range(chunks):
-        carried[:, chunk * width:(chunk + 1) * width] = dot3(
-            half, both(bq, slice(None), slice(chunk * width, (chunk + 1) * width)))
-
-        @pl.when(has_next)
-        def _(chunk=chunk):
-            k_copy(chunk).start()
-
     scaled[...] = dot3(split(dot3(both(ia), coupled)), both(ib))
     result = pltpu.make_async_copy(scaled, scaled_ref, local_sem.at[0])
     result.start()
@@ -265,9 +286,9 @@
     panel = pltpu.VMEM((block, outc), F32)
     scaled, earlier = pl.pallas_call(
         functools.partial(kernel, layers, n),
-        out_shape=[jax.ShapeDtypeStruct((block, outc), F32)] * 2,
+        out_shape=[pltpu.VMEM((block, outc), F32)] * 2,
         in_specs=[pl.BlockSpec(memory_space=pl.ANY)] * 6,
-        out_specs=[pl.BlockSpec(memory_space=pl.ANY)] * 2,
+        out_specs=[pl.BlockSpec(memory_space=pltpu.VMEM)] * 2,
         scratch_shapes=[
             pltpu.VMEM((n, tokens, block), BF16),
             pltpu.VMEM((block, n * tokens), BF16),
@@ -280,6 +301,8 @@
             pltpu.VMEM((2, outc, outc), BF16),
             pltpu.VMEM((2, block, block), BF16),
             pltpu.VMEM((2, block, block), BF16),
+            pltpu.VMEM((2, block, block), BF16),
+            pltpu.VMEM((2, outc, outc), BF16),
             pltpu.VMEM((2, outc, outc), BF16),
             pltpu.VMEM((2, outc, outc), BF16),
             panel, panel, panel, panel, panel,
@@ -289,7 +312,7 @@
             dma((chunks,)), dma((chunks,)), dma((chunks,)), dma((chunks,)),
         ],
         compiler_params=pltpu.CompilerParams(
-            collective_id=0, has_side_effects=True, vmem_limit_bytes=60 * 1024 * 1024),
+            collective_id=0, has_side_effects=True, vmem_limit_bytes=VMEM - 8 * block * outc - 65536),
     )(inputs, cotangents, input_factors, output_factors, input_coupling, output_coupling)
     return (scaled - earlier)[None]
 

time: 49.1 us -> 48 us (0.978)
  other arithmetic: 2.07 us -> 0.87 us
    broadcast_in_dim x1, other arithmetic: 2.07 us -> 0.87 us  [shards(): return (scaled - earlier)[None]]
where the time goes in v4:
time: 48 us; the launch traced here: 47.8 us
  Pallas kernels  47 us (98%)
  other arithmetic  0.87 us (2%)
    pallas_call x1, Pallas kernels, shards(): pl.pallas_call(functools.partial(kernel, layers, n), out_shape=[pltpu.VME...  47 us

profile of v4, /device:TPU:4, one launch (start us, length us, event | category | flops | bytes accessed | tf_op | source)
XLA Modules:
  0.0 47.8 jit_solution(13176975240576243778)
XLA Ops:
  0.0 47.0 %shard_map.64 = (f32[256,512]{1,0:T(8,128)S(1)}, f32[256,512]{1,0:T(8,128)S(1)}) custom-call(bf16[1,256,1024]{2,1,0:T(8,128)(2,1)} %x_ref.1, bf16[1,256,512]{2,1,0:T(8,128)(2,1)} %c_ref.1, f32[1,256,256]{2,1,0:T(8,128)} %a_ref.1, f32[1,512,512]{2,1,0:T(8,128)} %b_ref.1, f32[1,256,256]{2,1,0:T(8,128)} %p_ref.1, f32[1,512,512]{2,1,0:T(8,128)} %q_ref.1), custom_call_target="tpu_custom_call" | custom-call | tf_op jit(solution)/shard_map/pallas_call | solution.py:287
  47.0 0.9 %subtract_bitcast_fusion = f32[1,256,512]{2,1,0:T(8,128)} fusion(f32[256,512]{1,0:T(8,128)S(1)} %get-tuple-element.7, f32[256,512]{1,0:T(8,128)S(1)} %get-tuple-element.8), kind=kLoop, calls=%fused_computation | loop fusion | flops 131072 | bytes 1572864 | tf_op jit(solution)/shard_map/broadcast_in_dim | solution.py:317
